TPU v7x, 32 devices: a whole 2x2x4 slice. The times are simulated.
32 devices in a mesh: tm: 4 (over x, core), sky: 8 (over z, y).
Axes of the slice: x: 2, y: 2, z: 4, core: 2. Of those that a mesh axis runs over, the one named last changes fastest.
Arguments:
- residual: bfloat16 [64, 256, 2048], P('tm', 'sky'), may hold values from -6 to 6
- point_spread: bfloat16 [11, 11], replicated, may hold values from 0.0019989014 to 0.049804688
- star_row: int32 [2048], P('sky'), may hold values from 0 to 255, as said below
- star_col: int32 [2048], P('sky'), may hold values from 0 to 2047
- star_flux: float32 [2048], P('sky'), may hold values from 0.5 to 4
- transit_depth: float32 [2048], P('sky'), may hold values from 0.1 to 0.9
- transit_flag: int32 [64, 2048], P('tm', 'sky'), may hold values 0 or 1
Outputs:
- grid_grad: float32 [256, 2048], P('sky', 'tm')
- flux_grad: float32 [2048], P('sky')
- depth_grad: float32 [2048], P('sky')
Inputs may be any that keep to these rules, and one draw needn't show every extreme that they name: `star_row`: star s lies in rows (s // 256) * 32 to (s // 256) * 32 + 31.
All inputs are finite; a program needn't handle non-finite values. No bound on the sum of `transit_flag` on one device may be relied on, other than what follows from the above.
Results may differ from a plain program's by a relative error of at most 0.0003.
Values may be sent and summed in bfloat16 or wider, within the bound.
A program may use at most 320 MiB of HBM per device.

v0:
```python
import jax
import jax.numpy as jnp
from jax import lax
from jax.sharding import PartitionSpec as P


def extended(value, sides, width):
    for axis, dim in sides:
        size, length = (lax.axis_size(axis), value.shape[dim])
        up = [(i, (i + 1) % size) for i in range(size - 1)]
        down = [(j, i) for i, j in up]
        last = lax.slice_in_dim(value, length - width, length, axis=dim)
        initial = lax.slice_in_dim(value, 0, width, axis=dim)
        before = lax.ppermute(last, axis, up)
        after = lax.ppermute(initial, axis, down)
        value = jnp.concatenate([before, value, after], axis=dim)
    return value


def spread_tables(point_spread):
    width = point_spread.shape[0]
    margin = (width - 1) // 2
    spread = point_spread.astype(jnp.float32)
    inputs = lax.broadcasted_iota(jnp.int32, (128, 384, width), 0)
    columns = lax.broadcasted_iota(jnp.int32, (128, 384, width), 1)
    offsets = lax.broadcasted_iota(jnp.int32, (128, 384, width), 2)
    outputs = columns % 128
    block_step = columns // 128 - 1
    placed = (128 * block_step + inputs - outputs + margin == offsets).astype(jnp.float32)
    tables = jnp.einsum("ijk,dk->dij", placed, spread, precision=lax.Precision.HIGHEST)
    return tables.astype(jnp.bfloat16)


def correlate(source_grid, output_rows, tables):
    width = tables.shape[0]
    cadence_times, source_rows, column_count = source_grid.shape
    column_blocks = column_count // 128
    blocks = source_grid.reshape(cadence_times, source_rows, column_blocks, 128)
    summed = jnp.zeros((cadence_times, output_rows, column_blocks, 384), jnp.float32)
    for offset in range(width):
        row_slab = blocks[:, offset : offset + output_rows]
        summed = summed + jnp.einsum(
            "tnbi,ij->tnbj", row_slab, tables[offset], preferred_element_type=jnp.float32
        )
    from_left = summed[..., :128].reshape(cadence_times, output_rows, column_count)
    centre = summed[..., 128:256].reshape(cadence_times, output_rows, column_count)
    from_right = summed[..., 256:].reshape(cadence_times, output_rows, column_count)
    zero_block = jnp.zeros((cadence_times, output_rows, 128), jnp.float32)
    moved_left = jnp.concatenate([zero_block, from_left[:, :, : column_count - 128]], axis=2)
    moved_right = jnp.concatenate([from_right[:, :, 128:], zero_block], axis=2)
    return centre + moved_left + moved_right


def per_device(residual, point_spread, star_row, star_col, star_flux, transit_depth, transit_flag):
    margin = (point_spread.shape[0] - 1) // 2
    tables = spread_tables(point_spread)
    cadence_times, image_height, column_count = residual.shape
    padded = extended(residual, (("sky", 1),), margin)
    image = correlate(padded, image_height, tables)
    grid_local = jnp.sum(image, axis=0)
    local_row = star_row - lax.axis_index("sky") * image_height
    column_hot = (
        lax.broadcasted_iota(jnp.int32, (column_count, star_col.shape[0]), 0) == star_col[None, :]
    ).astype(jnp.float32)
    row_hot = (
        lax.broadcasted_iota(jnp.int32, (image_height, star_row.shape[0]), 0) == local_row[None, :]
    ).astype(jnp.float32)
    by_column = jnp.einsum("tyx,xs->tys", image, column_hot, precision=lax.Precision.HIGHEST)
    at_stars = jnp.sum(by_column * row_hot[None], axis=1)
    flags = transit_flag.astype(jnp.float32)
    flux_part = jnp.sum((1.0 - transit_depth[None, :] * flags) * at_stars, axis=0)
    flag_part = jnp.sum(flags * at_stars, axis=0)
    grid_share = lax.psum_scatter(grid_local, "tm", scatter_dimension=1, tiled=True)
    flux_total, flag_total = lax.psum((flux_part, flag_part), "tm")
    return (grid_share, flux_total, -star_flux * flag_total)


def solution(mesh):
    in_specs = (P("tm", "sky", None), P(), P("sky"), P("sky"), P("sky"), P("sky"), P("tm", "sky"))
    out_specs = (P("sky", "tm"), P("sky"), P("sky"))
    return jax.shard_map(
        per_device, mesh=mesh, in_specs=in_specs, out_specs=out_specs, check_vma=False
    )
```

profile of v0, /device:TPU:9, one launch (start us, length us, event | category | flops | bytes accessed | tf_op | source)
XLA Modules:
  0.0 218.7 jit_solution(14356330835958030666)
XLA Ops:
  7.2 2.3 %fusion.70 = (bf16[16,5,2048]{2,1,0:T(8,128)(2,1)}, bf16[16,5,2048]{2,1,0:T(8,128)(2,1)}) fusion(bf16[16,32,2048]{2,1,0:T(8,128)(2,1)} %param.7), kind=kLoop, calls=%fused_computation.77 | loop fusion | bytes 1310720 | tf_op jit(solution)/shard_map/slice | solution.py:12
  9.6 3.1 %collective-permute-start = (bf16[16,5,2048]{2,1,0:T(8,128)(2,1)}, bf16[16,5,2048]{2,1,0:T(8,128)(2,1)S(1)}, u32[]{:S(2)}, u32[]{:S(2)}) collective-permute-start(bf16[16,5,2048]{2,1,0:T(8,128)(2,1)} %get-tuple-element.10), channel_id=1, source_target_pairs={{0,1},{1,2},{2,3},{3,4},{4,5},{5,6},{6,7},{8,9},{9,10},{10,11},{11... | collective-permute-start | bytes 983048 | tf_op jit(solution)/shard_map/ppermute | solution.py:14
  12.7 3.0 %collective-permute-start.1 = (bf16[16,5,2048]{2,1,0:T(8,128)(2,1)}, bf16[16,5,2048]{2,1,0:T(8,128)(2,1)S(1)}, u32[]{:S(2)}, u32[]{:S(2)}) collective-permute-start(bf16[16,5,2048]{2,1,0:T(8,128)(2,1)} %get-tuple-element.11), channel_id=1, source_target_pairs={{1,0},{2,1},{3,2},{4,3},{5,4},{6,5},{7,6},{9,8},{10,9},{11,10},{12... | collective-permute-start | bytes 983048 | tf_op jit(solution)/shard_map/ppermute | solution.py:15
  15.8 1.1 fusion.14
  16.9 2.7 %fusion.71 = (bf16[1,128,384]{2,0,1:T(2,128)(2,1)S(1)}, bf16[1,128,384]{2,0,1:T(2,128)(2,1)S(1)}, bf16[1,128,384]{2,0,1:T(2,128)(2,1)}, bf16[1,128,384]{2,0,1:T(...) fusion(bf16[11,128,384]{2,0,1:T(8,128)(2,1)S(1)} %fusion.14), kind=kLoop, calls=%fused_computation.78 | loop fusion | bytes 2162688 | tf_op jit(solution)/shard_map/slice | solution.py:43
  19.6 0.6 fusion.57
  20.2 14.7 %collective-permute-done = bf16[16,5,2048]{2,1,0:T(8,128)(2,1)S(1)} collective-permute-done((bf16[16,5,2048]{2,1,0:T(8,128)(2,1)}, bf16[16,5,2048]{2,1,0:T(8,128)(2,1)S(1)}, u32[]{:S(2)}, u32[]{:S(2)}) %collective-permute-start) | collective-permute-done | bytes 327712 | tf_op jit(solution)/shard_map/ppermute | solution.py:14
  34.8 2.8 %collective-permute-done.1 = bf16[16,5,2048]{2,1,0:T(8,128)(2,1)S(1)} collective-permute-done((bf16[16,5,2048]{2,1,0:T(8,128)(2,1)}, bf16[16,5,2048]{2,1,0:T(8,128)(2,1)S(1)}, u32[]{:S(2)}, u32[]{:S(2)}) %collective-permute-start.1) | collective-permute-done | bytes 327712 | tf_op jit(solution)/shard_map/ppermute | solution.py:15
  37.6 3.2 %pad_maximum_fusion = bf16[16,42,2048]{2,1,0:T(8,128)(2,1)} fusion(bf16[16,5,2048]{2,1,0:T(8,128)(2,1)S(1)} %collective-permute-done.1, bf16[16,32,2048]{2,1,0:T(8,128)(2,1)S(1)} %copy-done.2, bf16[16,5,2048]{2,1,0:T(8,128)(2,1)S(1)} %collective-permute-done), kind=kLoop, calls=%fused_computation.2 | loop fusion | flops 8257536 | bytes 5505024 | tf_op jit(solution)/shard_map/concatenate | solution.py:16
  40.8 4.4 %reshape.57 = bf16[16,42,16,128]{3,2,1,0:T(8,128)(2,1)S(1)} reshape(bf16[16,42,2048]{2,1,0:T(8,128)(2,1)} %pad_maximum_fusion) | data formatting | bytes 5505024 | tf_op jit(solution)/shard_map/reshape | solution.py:38
  45.2 6.3 %fusion.28 = f32[16,32,16,384]{3,2,1,0:T(8,128)} fusion(bf16[16,42,16,128]{3,2,1,0:T(8,128)(2,1)S(1)} %reshape.57, bf16[1,128,384]{2,0,1:T(2,128)(2,1)S(1)} %copy-done.11), kind=kOutput, calls=%fused_computation.26 | convolution fusion | flops 805306368 | bytes 15433728 | tf_op jit(solution)/shard_map/tnbi,ij->tnbj/dot_general | solution.py:42
  51.5 6.3 %fusion.30 = f32[16,32,16,384]{3,2,1,0:T(8,128)} fusion(bf16[16,42,16,128]{3,2,1,0:T(8,128)(2,1)S(1)} %reshape.57, bf16[1,128,384]{2,0,1:T(2,128)(2,1)S(1)} %copy-done.10), kind=kOutput, calls=%fused_computation.28 | convolution fusion | flops 805306368 | bytes 15433728 | tf_op jit(solution)/shard_map/tnbi,ij->tnbj/dot_general | solution.py:42
  57.8 6.4 %fusion.32 = f32[16,32,16,384]{3,2,1,0:T(8,128)} fusion(bf16[16,42,16,128]{3,2,1,0:T(8,128)(2,1)S(1)} %reshape.57, bf16[1,128,384]{2,0,1:T(2,128)(2,1)S(1)} %copy-done.9), kind=kOutput, calls=%fused_computation.30 | convolution fusion | flops 805306368 | bytes 15433728 | tf_op jit(solution)/shard_map/tnbi,ij->tnbj/dot_general | solution.py:42
  64.2 6.2 %fusion.34 = f32[16,32,16,384]{3,2,1,0:T(8,128)} fusion(bf16[16,42,16,128]{3,2,1,0:T(8,128)(2,1)S(1)} %reshape.57, bf16[1,128,384]{2,0,1:T(2,128)(2,1)S(1)} %copy-done.8), kind=kOutput, calls=%fused_computation.32 | convolution fusion | flops 805306368 | bytes 15433728 | tf_op jit(solution)/shard_map/tnbi,ij->tnbj/dot_general | solution.py:42
  70.4 6.2 %fusion.36 = f32[16,32,16,384]{3,2,1,0:T(8,128)} fusion(bf16[16,42,16,128]{3,2,1,0:T(8,128)(2,1)S(1)} %reshape.57, bf16[1,128,384]{2,0,1:T(2,128)(2,1)S(1)} %copy-done.7), kind=kOutput, calls=%fused_computation.34 | convolution fusion | flops 805306368 | bytes 15433728 | tf_op jit(solution)/shard_map/tnbi,ij->tnbj/dot_general | solution.py:42
  76.7 6.3 %fusion.38 = f32[16,32,16,384]{3,2,1,0:T(8,128)} fusion(bf16[16,42,16,128]{3,2,1,0:T(8,128)(2,1)S(1)} %reshape.57, bf16[1,128,384]{2,0,1:T(2,128)(2,1)S(1)} %copy-done.6), kind=kOutput, calls=%fused_computation.36 | convolution fusion | flops 805306368 | bytes 15433728 | tf_op jit(solution)/shard_map/tnbi,ij->tnbj/dot_general | solution.py:42
  82.9 6.3 %fusion.40 = f32[16,32,16,384]{3,2,1,0:T(8,128)} fusion(bf16[16,42,16,128]{3,2,1,0:T(8,128)(2,1)S(1)} %reshape.57, bf16[1,128,384]{2,0,1:T(2,128)(2,1)S(1)} %copy-done.5), kind=kOutput, calls=%fused_computation.38 | convolution fusion | flops 805306368 | bytes 15433728 | tf_op jit(solution)/shard_map/tnbi,ij->tnbj/dot_general | solution.py:42
  89.2 6.6 %fusion.42 = f32[16,32,16,384]{3,2,1,0:T(8,128)} fusion(bf16[16,42,16,128]{3,2,1,0:T(8,128)(2,1)S(1)} %reshape.57, bf16[1,128,384]{2,0,1:T(2,128)(2,1)S(1)} %copy-done.4), kind=kOutput, calls=%fused_computation.40 | convolution fusion | flops 805306368 | bytes 15433728 | tf_op jit(solution)/shard_map/tnbi,ij->tnbj/dot_general | solution.py:42
  95.8 6.3 %fusion.44 = f32[16,32,16,384]{3,2,1,0:T(8,128)} fusion(bf16[16,42,16,128]{3,2,1,0:T(8,128)(2,1)S(1)} %reshape.57, bf16[1,128,384]{2,0,1:T(2,128)(2,1)S(1)} %copy-done.3), kind=kOutput, calls=%fused_computation.42 | convolution fusion | flops 805306368 | bytes 15433728 | tf_op jit(solution)/shard_map/tnbi,ij->tnbj/dot_general | solution.py:42
  102.1 6.3 %fusion.26 = f32[16,32,16,384]{3,2,1,0:T(8,128)} fusion(bf16[16,42,16,128]{3,2,1,0:T(8,128)(2,1)S(1)} %reshape.57, bf16[1,128,384]{2,0,1:T(2,128)(2,1)S(1)} %get-tuple-element.13), kind=kOutput, calls=%fused_computation.24 | convolution fusion | flops 805306368 | bytes 15433728 | tf_op jit(solution)/shard_map/tnbi,ij->tnbj/dot_general | solution.py:42
  108.4 44.4 %add_add_fusion = f32[16,32,16,384]{3,2,1,0:T(8,128)} fusion(f32[16,32,16,384]{3,2,1,0:T(8,128)} %fusion.26, f32[16,32,16,384]{3,2,1,0:T(8,128)} %fusion.28, f32[16,32,16,384]{3,2,1,0:T(8,128)} %fusion.30, f32[16,32,16,384]{3,2,1,0:T(8,128)} %fusion.32, f32[16,32,16,384]{3,2,1,0:T(8,128)} %fusion.34, f32[16,32,16,384]{3,2,1,0:T(8,128)} %fusion.36, ...), kind=kOutput, calls=%fused_computation | convolution fusion | flops 836763648 | bytes 141262848 | tf_op jit(solution)/shard_map/tnbi,ij->tnbj/dot_general | solution.py:42
  152.8 9.6 %fusion.69 = (f32[16,32,16,128]{3,2,1,0:T(8,128)}, f32[16,32,16,128]{3,2,1,0:T(8,128)}, f32[16,32,16,128]{3,2,1,0:T(8,128)}) fusion(f32[16,32,16,384]{3,2,1,0:T(8,128)} %add_add_fusion), kind=kLoop, calls=%fused_computation.76 | loop fusion | bytes 25165824 | tf_op jit(solution)/shard_map/slice | solution.py:45
  162.3 4.9 %reshape.42 = f32[16,32,2048]{2,1,0:T(8,128)} reshape(f32[16,32,16,128]{3,2,1,0:T(8,128)} %get-tuple-element.7) | data formatting | bytes 8388608 | tf_op jit(solution)/shard_map/reshape | solution.py:45
  167.2 4.2 %slice.129 = f32[16,32,1920]{2,1,0:T(8,128)} slice(f32[16,32,2048]{2,1,0:T(8,128)} %reshape.42), slice={[0:16], [0:32], [0:1920]} | slice | bytes 7864320 | tf_op jit(solution)/shard_map/slice | solution.py:49
  171.5 4.9 %reshape.43 = f32[16,32,2048]{2,1,0:T(8,128)} reshape(f32[16,32,16,128]{3,2,1,0:T(8,128)} %get-tuple-element.8) | data formatting | bytes 8388608 | tf_op jit(solution)/shard_map/reshape | solution.py:47
  176.4 4.3 %slice.131 = f32[16,32,1920]{2,1,0:T(8,128)} slice(f32[16,32,2048]{2,1,0:T(8,128)} %reshape.43), slice={[0:16], [0:32], [128:2048]} | slice | bytes 7864320 | tf_op jit(solution)/shard_map/slice | solution.py:50
  180.7 4.9 %reshape.41 = f32[16,32,2048]{2,1,0:T(8,128)} reshape(f32[16,32,16,128]{3,2,1,0:T(8,128)} %get-tuple-element.9) | data formatting | bytes 8388608 | tf_op jit(solution)/shard_map/reshape | solution.py:46
  185.6 6.1 %fusion.68 = f32[32,2048]{1,0:T(8,128)} fusion(f32[16,32,1920]{2,1,0:T(8,128)} %slice.131, f32[16,32,2048]{2,1,0:T(8,128)} %reshape.41, f32[16,32,1920]{2,1,0:T(8,128)} %slice.129), kind=kLoop, calls=%fused_computation.75 | loop fusion | flops 3080192 | bytes 12320768 | tf_op jit(solution)/shard_map/reduce_sum | solution.py:60
  191.7 7.0 %fusion.18 = f32[16,256]{1,0:T(8,128)S(1)} fusion(s32[256]{0:T(256)S(1)} %copy-done.14, f32[32,256]{1,0:T(8,128)S(1)} %copy-done.12, f32[16,32,1920]{2,1,0:T(8,128)} %slice.131, f32[16,32,2048]{2,1,0:T(8,128)} %reshape.41, f32[16,32,1920]{2,1,0:T(8,128)} %slice.129), kind=kOutput, calls=%fused_computation.20 | convolution fusion | flops 3224104960 | bytes 12108800 | tf_op jit(solution)/shard_map/tyx,xs->tys/dot_general | solution.py:68
  198.8 6.1 %all-reduce.2 = (f32[256]{0:T(256)}, f32[256]{0:T(256)S(1)}) all-reduce(f32[256]{0:T(256)S(1)} %get-tuple-element.4, f32[256]{0:T(256)S(1)} %get-tuple-element.3), channel_id=1, replica_groups=mesh['tm'=4,'sky'=8] {'tm'}, use_global_device_ids=true, to_apply=%region_4.5 | all-reduce | flops 512 | bytes 4096 | tf_op jit(solution)/shard_map/psum | solution.py:74
  204.9 0.6 negate_multiply_fusion
  205.5 6.3 %reduce-scatter.2.cloned.1.call-done = f32[32,512]{1,0:T(8,128)} async-done(((f32[32,2048]{1,0:T(8,128)}), f32[32,512]{1,0:T(8,128)}) %reduce-scatter.2.cloned.1.call-update) | async-done | bytes 65552 | tf_op jit(solution)/shard_map/reduce_scatter | solution.py:73
  (43 shorter events, 0.2 us)
Async XLA Ops:
  7.2 8.6 %copy-start = (bf16[11,11]{1,0:T(8,128)(2,1)S(1)}, bf16[11,11]{1,0:T(8,128)(2,1)}, u32[]{:S(2)}) copy-start(bf16[11,11]{1,0:T(8,128)(2,1)} %param.8) | copy-start | bytes 730
  7.2 204.6 %reduce-scatter.2.cloned.1.call-start = ((), (), s32[]{:S(2)}) async-start(), calls=%async_computation.1 | async-start | bytes 327680 | tf_op jit(solution)/shard_map/reduce_scatter | solution.py:73
  9.6 25.3 %collective-permute-start = (bf16[16,5,2048]{2,1,0:T(8,128)(2,1)}, bf16[16,5,2048]{2,1,0:T(8,128)(2,1)S(1)}, u32[]{:S(2)}, u32[]{:S(2)}) collective-permute-start(bf16[16,5,2048]{2,1,0:T(8,128)(2,1)} %get-tuple-element.10), channel_id=1, source_target_pairs={{0,1},{1,2},{2,3},{3,4},{4,5},{5,6},{6,7},{8,9},{9,10},{10,11},{11... | collective-permute-start | bytes 983048 | tf_op jit(solution)/shard_map/ppermute | solution.py:14
  12.7 24.9 %collective-permute-start.1 = (bf16[16,5,2048]{2,1,0:T(8,128)(2,1)}, bf16[16,5,2048]{2,1,0:T(8,128)(2,1)S(1)}, u32[]{:S(2)}, u32[]{:S(2)}) collective-permute-start(bf16[16,5,2048]{2,1,0:T(8,128)(2,1)} %get-tuple-element.11), channel_id=1, source_target_pairs={{1,0},{2,1},{3,2},{4,3},{5,4},{6,5},{7,6},{9,8},{10,9},{11,10},{12... | collective-permute-start | bytes 983048 | tf_op jit(solution)/shard_map/ppermute | solution.py:15
  16.9 2.7 %copy-start.17 = (s32[256]{0:T(256)S(1)}, s32[256]{0:T(256)}, u32[]{:S(2)}) copy-start(s32[256]{0:T(256)} %param.9) | copy-start | bytes 3076
  16.9 20.8 %copy-start.2 = (bf16[16,32,2048]{2,1,0:T(8,128)(2,1)S(1)}, bf16[16,32,2048]{2,1,0:T(8,128)(2,1)}, u32[]{:S(2)}) copy-start(bf16[16,32,2048]{2,1,0:T(8,128)(2,1)} %param.7) | copy-start | bytes 6291460
  40.8 4.4 %copy-start.11 = (bf16[1,128,384]{2,0,1:T(2,128)(2,1)S(1)}, bf16[1,128,384]{2,0,1:T(2,128)(2,1)}, u32[]{:S(2)}) copy-start(bf16[1,128,384]{2,0,1:T(2,128)(2,1)} %get-tuple-element.14) | copy-start | bytes 294916
  45.2 6.3 %copy-start.10 = (bf16[1,128,384]{2,0,1:T(2,128)(2,1)S(1)}, bf16[1,128,384]{2,0,1:T(2,128)(2,1)}, u32[]{:S(2)}) copy-start(bf16[1,128,384]{2,0,1:T(2,128)(2,1)} %get-tuple-element.15) | copy-start | bytes 294916
  51.5 6.3 %copy-start.9 = (bf16[1,128,384]{2,0,1:T(2,128)(2,1)S(1)}, bf16[1,128,384]{2,0,1:T(2,128)(2,1)}, u32[]{:S(2)}) copy-start(bf16[1,128,384]{2,0,1:T(2,128)(2,1)} %get-tuple-element.16) | copy-start | bytes 294916
  57.8 6.4 %copy-start.8 = (bf16[1,128,384]{2,0,1:T(2,128)(2,1)S(1)}, bf16[1,128,384]{2,0,1:T(2,128)(2,1)}, u32[]{:S(2)}) copy-start(bf16[1,128,384]{2,0,1:T(2,128)(2,1)} %get-tuple-element.17) | copy-start | bytes 294916
  64.2 6.3 %copy-start.7 = (bf16[1,128,384]{2,0,1:T(2,128)(2,1)S(1)}, bf16[1,128,384]{2,0,1:T(2,128)(2,1)}, u32[]{:S(2)}) copy-start(bf16[1,128,384]{2,0,1:T(2,128)(2,1)} %get-tuple-element.18) | copy-start | bytes 294916
  70.4 6.2 %copy-start.6 = (bf16[1,128,384]{2,0,1:T(2,128)(2,1)S(1)}, bf16[1,128,384]{2,0,1:T(2,128)(2,1)}, u32[]{:S(2)}) copy-start(bf16[1,128,384]{2,0,1:T(2,128)(2,1)} %get-tuple-element.19) | copy-start | bytes 294916
  76.7 6.3 %copy-start.5 = (bf16[1,128,384]{2,0,1:T(2,128)(2,1)S(1)}, bf16[1,128,384]{2,0,1:T(2,128)(2,1)}, u32[]{:S(2)}) copy-start(bf16[1,128,384]{2,0,1:T(2,128)(2,1)} %get-tuple-element.20) | copy-start | bytes 294916
  82.9 6.3 %copy-start.4 = (bf16[1,128,384]{2,0,1:T(2,128)(2,1)S(1)}, bf16[1,128,384]{2,0,1:T(2,128)(2,1)}, u32[]{:S(2)}) copy-start(bf16[1,128,384]{2,0,1:T(2,128)(2,1)} %get-tuple-element.21) | copy-start | bytes 294916
  89.2 6.6 %copy-start.3 = (bf16[1,128,384]{2,0,1:T(2,128)(2,1)S(1)}, bf16[1,128,384]{2,0,1:T(2,128)(2,1)}, u32[]{:S(2)}) copy-start(bf16[1,128,384]{2,0,1:T(2,128)(2,1)} %get-tuple-element.22) | copy-start | bytes 294916
  185.6 6.1 %copy-start.12 = (f32[32,256]{1,0:T(8,128)S(1)}, f32[32,256]{1,0:T(8,128)}, u32[]{:S(2)}) copy-start(f32[32,256]{1,0:T(8,128)} %fusion.57) | copy-start | bytes 98308
  185.6 6.1 %copy-start.14 = (s32[256]{0:T(256)S(1)}, s32[256]{0:T(256)}, u32[]{:S(2)}) copy-start(s32[256]{0:T(256)} %param.10) | copy-start | bytes 3076
  191.7 7.1 %copy-start.13 = (s32[16,256]{1,0:T(8,128)S(1)}, s32[16,256]{1,0:T(8,128)}, u32[]{:S(2)}) copy-start(s32[16,256]{1,0:T(8,128)} %param.13) | copy-start | bytes 49156
  191.7 7.1 %copy-start.15 = (f32[256]{0:T(256)S(1)}, f32[256]{0:T(256)}, u32[]{:S(2)}) copy-start(f32[256]{0:T(256)} %param.12) | copy-start | bytes 3076
  191.7 13.2 %copy-start.16 = (f32[256]{0:T(256)S(1)}, f32[256]{0:T(256)}, u32[]{:S(2)}) copy-start(f32[256]{0:T(256)} %param.11) | copy-start | bytes 3076
  191.7 20.1 %copy-start.1 = (bf16[11,11]{1,0:T(8,128)(2,1)S(1)}, bf16[11,11]{1,0:T(8,128)(2,1)}, u32[]{:S(2)}) copy-start(bf16[11,11]{1,0:T(8,128)(2,1)} %param.8) | copy-start | bytes 730
Sparse Core Ops, SparseCore 0:
  191.8 19.9 reduce-scatter.1
where the time goes:
time: 221 us; the launch traced here: 219 us
  matrix products  116 us (52%)
  local copies, waits for them, and re-layouts  42.3 us (19%)
  waiting for transfers between devices  23.8 us (11%)
  between operations  14.2 us (6%)
  other arithmetic  10.4 us (5%)
  starting transfers between devices  6.21 us (3%)
  blocking collectives  6.07 us (3%)
    dot_general x11, matrix products, correlate(): jnp.einsum('tnbi,ij->tnbj', row_slab, tables[offset], preferred_element_t...  108 us
    ppermute x1, waiting for transfers between devices, extended(): before = lax.ppermute(last, axis, up)  14.7 us
    slice x1, local copies, waits for them, and re-layouts, correlate(): summed[..., :128].reshape(cadence_times, output_rows, column_count)  9.55 us
    dot_general x1, matrix products, per_device(): jnp.einsum('tyx,xs->tys', image, column_hot, precision=lax.Precision.HIGH...  7.04 us
    reduce_scatter x1, waiting for transfers between devices, per_device(): lax.psum_scatter(grid_local, 'tm', scatter_dimension=1, tiled=True)  6.34 us
    psum x1, blocking collectives, per_device(): flux_total, flag_total = lax.psum((flux_part, flag_part), 'tm')  6.07 us
    reduce_sum x1, other arithmetic, per_device(): grid_local = jnp.sum(image, axis=0)  6.07 us
    reshape x1, local copies, waits for them, and re-layouts, correlate(): summed[..., 256:].reshape(cadence_times, output_rows, column_count)  4.92 us
  transfers between devices with their start and end apart: 3, of which 3 were waited for; matrix products, arithmetic and copies ran while one was open for 5% of the time, Pallas kernels for 0%

commit v1 on v0

v1 whole, which is shorter than its diff:
```python
import functools
import jax
import jax.numpy as jnp
from jax import lax
from jax.experimental import pallas as pl
from jax.experimental.pallas import tpu as pltpu
from jax.sharding import PartitionSpec as P

LANES = 128
PAD = 8


def local_kernel(
    stars_ref, psf_ref, res_ref, flags_ref, grid_ref, part_ref,
    flat, windows, table, wide, gathered, dense, summed, split,
):
    times, rows, columns = res_ref.shape
    width = psf_ref.shape[0]
    margin = (width - 1) // 2
    blocks = columns // LANES
    halves = rows // 16
    star_count = stars_ref.shape[1]
    tall = rows + 2 * margin

    span = 144
    gap = lax.broadcasted_iota(jnp.int32, (span, LANES), 0) - lax.broadcasted_iota(
        jnp.int32, (span, LANES), 1
    )
    for a in range(width):
        entry = jnp.zeros((span, LANES), jnp.float32)
        for b in range(width):
            entry = jnp.where(gap == b, psf_ref[a, b], entry)
        entry = entry.astype(jnp.bfloat16)
        table[pl.ds(a * LANES, LANES), :] = entry[:LANES]
        wide[pl.ds(0, span), pl.ds(a * LANES, LANES)] = entry
    wide[pl.ds(span, 256 - span), :] = jnp.zeros((256 - span, width * LANES), jnp.bfloat16)

    zero_side = jnp.zeros((rows, LANES), jnp.float32)
    summed[:, pl.ds(0, LANES)] = zero_side
    summed[:, pl.ds(LANES + columns, LANES)] = zero_side
    summed[:, pl.ds(2 * LANES + columns, LANES)] = zero_side

    @pl.loop(0, blocks)
    def _(b):
        at = pl.ds(pl.multiple_of(b * LANES, LANES), LANES)
        total = res_ref[0, :, at].astype(jnp.float32)
        for t in range(1, times):
            total = total + res_ref[t, :, at].astype(jnp.float32)
        summed[:, pl.ds(pl.multiple_of((b + 1) * LANES, LANES), LANES)] = total

    grid_ref[...] = jnp.zeros_like(grid_ref)
    group = 4

    @pl.loop(0, blocks // group)
    def _(g):
        for i in range(group):
            start = pl.multiple_of((g * group + i) * LANES, LANES)
            window = summed[:, pl.ds(start, 3 * LANES)]
            moved = pltpu.roll(window, margin, 1)[:, LANES:]
            high = moved.astype(jnp.bfloat16)
            low = (moved - high.astype(jnp.float32)).astype(jnp.bfloat16)
            split[pl.ds(2 * i * rows, rows), :] = high
            split[pl.ds((2 * i + 1) * rows, rows), :] = low
        for a in range(width):
            product = jnp.dot(
                split[...], wide[:, pl.ds(a * LANES, LANES)], preferred_element_type=jnp.float32
            )
            for i in range(group):
                start = pl.multiple_of((g * group + i) * LANES, LANES)
                term = product[2 * i * rows : (2 * i + 1) * rows] + product[
                    (2 * i + 1) * rows : (2 * i + 2) * rows
                ]
                grid_ref[pl.ds(PAD + margin - a, rows), pl.ds(start, LANES)] += term

    flat[:, pl.ds(0, LANES)] = jnp.zeros((256, LANES), jnp.float32)
    flat[:, pl.ds(LANES + columns, LANES)] = jnp.zeros((256, LANES), jnp.float32)
    first = lax.broadcasted_iota(jnp.int32, (256, 256), 0)
    second = lax.broadcasted_iota(jnp.int32, (256, 256), 1)
    swap = (first == (second % 16) * 16 + second // 16).astype(jnp.bfloat16)
    windows[:, pl.ds(0, margin)] = jnp.zeros((2 * blocks, margin, 16, LANES), jnp.bfloat16)
    windows[:, pl.ds(margin + rows, margin)] = jnp.zeros(
        (2 * blocks, margin, 16, LANES), jnp.bfloat16
    )
    for h in range(halves):

        @pl.loop(0, columns // 256)
        def _(c):
            at = pl.ds(pl.multiple_of(c * 256, 256), 256)
            piece = res_ref[:, pl.ds(16 * h, 16), at].reshape(256, 256)
            flat[:, pl.ds(pl.multiple_of(c * 256 + LANES, LANES), 256)] = jnp.dot(
                swap, piece, preferred_element_type=jnp.float32
            )

        @pl.loop(0, blocks)
        def _(b):
            start = pl.multiple_of(b * LANES, LANES)
            left = flat[:, pl.ds(start, 2 * LANES)]
            right = flat[:, pl.ds(pl.multiple_of(start + LANES, LANES), 2 * LANES)]
            near = pltpu.roll(left, margin, 1)[:, LANES:]
            far = pltpu.roll(right, 2 * LANES - (64 - margin), 1)[:, :LANES]
            rows_at = pl.ds(margin + 16 * h, 16)
            windows[b, rows_at] = near.astype(jnp.bfloat16).reshape(16, 16, LANES)
            windows[blocks + b, rows_at] = far.astype(jnp.bfloat16).reshape(16, 16, LANES)

    lane = lax.broadcasted_iota(jnp.int32, (16, LANES), 1)
    lowest = lax.axis_index("sky") * rows
    for which, (first_tap, taps) in enumerate(((0, width), (width - margin, margin), (0, margin))):
        base = first_tap
        last = tall - taps

        def chunk(g, c, slot, acc):
            for s in range(16):
                star = g * LANES + c * 16 + s
                row = stars_ref[2 * which, star] - lowest + base
                row = jnp.clip(row, 0, last)
                column = stars_ref[2 * which + 1, star]
                block = column // LANES + blocks * ((column // 64) % 2)
                found = windows[block, pl.ds(row, taps)]
                for a in range(taps):
                    gathered[slot, pl.ds(16 * s, 16), pl.ds(a * LANES, LANES)] = found[a]
            dense[slot] = jnp.dot(
                gathered[slot, :, pl.ds(0, taps * LANES)],
                table[pl.ds(first_tap * LANES, taps * LANES), :],
                preferred_element_type=jnp.float32,
            )
            for s in range(16):
                star = g * LANES + c * 16 + s
                place = c * 16 + s
                offset = stars_ref[2 * which + 1, star] % 64
                moved = pltpu.roll(
                    dense[slot, pl.ds(16 * s, 16), :], (place - offset + LANES) % LANES, 1
                )
                acc = jnp.where(lane == place, moved, acc)
            return acc

        for g in range(star_count // LANES):

            def pair(c, acc, g=g):
                acc = chunk(g, 2 * c, 0, acc)
                return chunk(g, 2 * c + 1, 1, acc)

            acc = lax.fori_loop(0, LANES // 32, pair, jnp.zeros((16, LANES), jnp.float32))
            at = pl.ds(g * LANES, LANES)
            part_ref[pl.ds(2 * which, 1), at] = jnp.sum(acc, axis=0, keepdims=True)
            part_ref[pl.ds(2 * which + 1, 1), at] = jnp.sum(
                acc * flags_ref[which, :, at], axis=0, keepdims=True
            )


def local_parts(stars, spread, residual, flags):
    times, rows, columns = residual.shape
    width = spread.shape[0]
    margin = (width - 1) // 2
    blocks = columns // LANES
    count = stars.shape[1]
    vmem = pl.BlockSpec(memory_space=pltpu.VMEM)
    smem = pl.BlockSpec(memory_space=pltpu.SMEM)
    return pl.pallas_call(
        local_kernel,
        out_shape=(
            jax.ShapeDtypeStruct((rows + 2 * PAD, columns), jnp.float32),
            jax.ShapeDtypeStruct((8, count), jnp.float32),
        ),
        in_specs=[smem, smem, vmem, vmem],
        out_specs=(vmem, vmem),
        scratch_shapes=[
            pltpu.VMEM((256, columns + 2 * LANES), jnp.float32),
            pltpu.VMEM((2 * blocks, rows + 2 * margin, 16, LANES), jnp.bfloat16),
            pltpu.VMEM((width * LANES, LANES), jnp.bfloat16),
            pltpu.VMEM((256, width * LANES), jnp.bfloat16),
            pltpu.VMEM((2, 256, width * LANES), jnp.bfloat16),
            pltpu.VMEM((2, 256, LANES), jnp.float32),
            pltpu.VMEM((rows, columns + 3 * LANES), jnp.float32),
            pltpu.VMEM((8 * rows, 256), jnp.bfloat16),
        ],
        compiler_params=pltpu.CompilerParams(vmem_limit_bytes=40 << 20),
    )(stars, spread, residual, flags)


def per_device(residual, point_spread, star_row, star_col, star_flux, transit_depth, transit_flag):
    times, rows, columns = residual.shape
    size = lax.axis_size("sky")
    up = [(i, i + 1) for i in range(size - 1)]
    down = [(i + 1, i) for i in range(size - 1)]
    info = jnp.concatenate([star_row[None], star_col[None], transit_flag], axis=0)
    before = lax.ppermute(info, "sky", up)
    after = lax.ppermute(info, "sky", down)
    stars = jnp.concatenate([info[:2], before[:2], after[:2]], axis=0)
    flags = jnp.stack([info[2:], before[2:], after[2:]]).astype(jnp.float32)
    grid, part = local_parts(stars, point_spread.astype(jnp.float32), residual, flags)
    edge_count = PAD * columns
    to_before = jnp.concatenate([grid[:PAD].reshape(-1), part[2:4].reshape(-1)])
    to_after = jnp.concatenate([grid[PAD + rows :].reshape(-1), part[4:6].reshape(-1)])
    from_before = lax.ppermute(to_after, "sky", up)
    from_after = lax.ppermute(to_before, "sky", down)
    own = grid[PAD : PAD + rows]
    own = own.at[:PAD].add(from_before[:edge_count].reshape(PAD, columns))
    own = own.at[rows - PAD :].add(from_after[:edge_count].reshape(PAD, columns))
    sums = part[:2] + (from_before[edge_count:] + from_after[edge_count:]).reshape(2, -1)
    grid_share = lax.psum_scatter(own, "tm", scatter_dimension=1, tiled=True)
    sums = lax.psum(sums, "tm")
    return (grid_share, sums[0] - transit_depth * sums[1], -star_flux * sums[1])


def solution(mesh):
    in_specs = (P("tm", "sky", None), P(), P("sky"), P("sky"), P("sky"), P("sky"), P("tm", "sky"))
    out_specs = (P("sky", "tm"), P("sky"), P("sky"))
    return jax.shard_map(
        per_device, mesh=mesh, in_specs=in_specs, out_specs=out_specs, check_vma=False
    )
```

time: 221 us -> 95.3 us (0.43)
  the two profiles are of different devices: /device:TPU:9 before, /device:TPU:0 now
where the time goes in v1:
time: 95.3 us; the launch traced here: 94.9 us
  Pallas kernels  33.7 us (35%)
  waiting for transfers between devices  22.4 us (24%)
  between operations  14.2 us (15%)
  starting transfers between devices  13 us (14%)
  blocking collectives  5.67 us (6%)
  other arithmetic  3.49 us (4%)
  local copies, waits for them, and re-layouts  2.46 us (3%)
    pallas_call x1, Pallas kernels, local_parts(): pl.pallas_call(local_kernel, out_shape=(jax.ShapeDtypeStruct((rows + 2 *...  33.7 us
    reduce_scatter x1, waiting for transfers between devices, per_device(): grid_share = lax.psum_scatter(own, 'tm', scatter_dimension=1, tiled=True)  15.6 us
    psum x1, blocking collectives, per_device(): sums = lax.psum(sums, 'tm')  5.67 us
    ppermute x1, starting transfers between devices, per_device(): before = lax.ppermute(info, 'sky', up)  5.5 us
    ppermute x1, waiting for transfers between devices, per_device(): from_after = lax.ppermute(to_before, 'sky', down)  5.44 us
    ppermute x1, starting transfers between devices, per_device(): from_before = lax.ppermute(to_after, 'sky', up)  4.84 us
    unnamed x14, local copies, waits for them, and re-layouts  2.35 us
  transfers between devices with their start and end apart: 5, of which 4 were waited for; matrix products, arithmetic and copies ran while one was open for 1% of the time, Pallas kernels for 0%

profile of v1, /device:TPU:0, one launch (start us, length us, event | category | flops | bytes accessed | tf_op | source)
XLA Modules:
  0.0 94.9 jit_solution(7323470898139378427)
XLA Ops:
  7.2 0.0 reduce-scatter.2.cloned.1.call-start
  7.2 0.7 pad_add_fusion
  8.0 1.3 %collective-permute-start.1 = (s32[18,256]{1,0:T(8,128)S(1)}, s32[18,256]{1,0:T(8,128)S(1)}, u32[]{:S(2)}, u32[]{:S(2)}) collective-permute-start(s32[18,256]{1,0:T(8,128)S(1)} %pad_add_fusion), channel_id=1, source_target_pairs={{1,0},{2,1},{3,2},{4,3},{5,4},{6,5},{7,6},{9,8},{10,9},{11,10},{12... | collective-permute-start | bytes 55304 | tf_op jit(solution)/shard_map/ppermute | solution.py:187
  9.2 5.5 %collective-permute-start = (s32[18,256]{1,0:T(8,128)S(1)}, s32[18,256]{1,0:T(8,128)S(1)}, u32[]{:S(2)}, u32[]{:S(2)}) collective-permute-start(s32[18,256]{1,0:T(8,128)S(1)} %pad_add_fusion), channel_id=1, source_target_pairs={{0,1},{1,2},{2,3},{3,4},{4,5},{5,6},{6,7},{8,9},{9,10},{10,11},{11... | collective-permute-start | bytes 55304 | tf_op jit(solution)/shard_map/ppermute | solution.py:186
  14.8 0.7 convert_element_type.6.psf_ref
  15.4 0.0 collective-permute-done.1
  15.5 0.8 collective-permute-done
  16.3 0.7 pad_add_fusion.1.stars_ref
  17.0 0.7 add_convert_fusion.flags_ref
  17.7 0.0 copy-start
  17.7 1.6 %copy-done = bf16[16,32,2048]{2,1,0:T(8,128)(2,1)S(1)} copy-done((bf16[16,32,2048]{2,1,0:T(8,128)(2,1)S(1)}, bf16[16,32,2048]{2,1,0:T(8,128)(2,1)}, u32[]{:S(2)}) %copy-start) | copy-done | bytes 2097176
  19.3 0.0 copy-start.2
  19.3 0.0 copy-start.3
  19.3 33.7 %shard_map.94 = (f32[48,2048]{1,0:T(8,128)S(1)}, f32[8,256]{1,0:T(8,128)S(1)}) custom-call(s32[6,256]{1,0:T(8,128)S(1)} %pad_add_fusion.1.stars_ref, f32[11,11]{1,0:T(8,128)S(1)} %convert_element_type.6.psf_ref, bf16[16,32,2048]{2,1,0:T(8,128)(2,1)S(1)} %copy-done, f32[3,16,256]{2,1,0:T(8,128)S(1)} %add_convert_fusion.flags_ref), custom_call_target="tpu_custom_call" | custom-call | tf_op jit(solution)/shard_map/pallas_call | solution.py:158
  53.1 4.8 %collective-permute-start.2 = (f32[16896]{0:T(1024)S(1)}, f32[16896]{0:T(1024)S(1)}, u32[]{:S(2)}, u32[]{:S(2)}) collective-permute-start(f32[16896]{0:T(1024)S(1)} %pad_maximum_fusion), channel_id=1, source_target_pairs={{0,1},{1,2},{2,3},{3,4},{4,5},{5,6},{6,7},{8,9},{9,10},{10,11},{11... | collective-permute-start | bytes 202760 | tf_op jit(solution)/shard_map/ppermute | solution.py:194
  58.0 1.3 %collective-permute-start.3 = (f32[16896]{0:T(1024)S(1)}, f32[16896]{0:T(1024)S(1)}, u32[]{:S(2)}, u32[]{:S(2)}) collective-permute-start(f32[16896]{0:T(1024)S(1)} %pad_maximum_fusion.1), channel_id=1, source_target_pairs={{1,0},{2,1},{3,2},{4,3},{5,4},{6,5},{7,6},{9,8},{10,9},{11,10},{12... | collective-permute-start | bytes 202760 | tf_op jit(solution)/shard_map/ppermute | solution.py:195
  59.3 0.6 collective-permute-done.2
  59.9 5.4 %collective-permute-done.3 = f32[16896]{0:T(1024)S(1)} collective-permute-done((f32[16896]{0:T(1024)S(1)}, f32[16896]{0:T(1024)S(1)}, u32[]{:S(2)}, u32[]{:S(2)}) %collective-permute-start.3) | collective-permute-done | bytes 67616 | tf_op jit(solution)/shard_map/ppermute | solution.py:195
  65.5 0.0 copy-start.1
  65.5 0.7 copy-done.1
  66.2 0.0 reduce-scatter.2.cloned.1.call-update
  66.2 5.7 %psum.7 = f32[2,256]{1,0:T(2,128)S(1)} all-reduce(f32[2,256]{1,0:T(2,128)S(1)} %slice_add_fusion.2), channel_id=1, replica_groups=mesh['tm'=4,'sky'=8] {'tm'}, use_global_device_ids=true, to_apply=%region_1.0 | all-reduce | flops 512 | bytes 4096 | tf_op jit(solution)/shard_map/psum | solution.py:201
  71.9 0.0 copy-done.2
  71.9 0.0 copy-done.3
  71.9 0.6 negate_multiply_fusion
  72.5 15.6 %reduce-scatter.2.cloned.1.call-done = f32[32,512]{1,0:T(8,128)} async-done(((f32[32,2048]{1,0:T(8,128)}), f32[32,512]{1,0:T(8,128)}) %reduce-scatter.2.cloned.1.call-update) | async-done | bytes 65552 | tf_op jit(solution)/shard_map/reduce_scatter | solution.py:200
  (23 shorter events, 0.2 us)
Async XLA Ops:
  7.2 80.9 %reduce-scatter.2.cloned.1.call-start = ((), (), s32[]{:S(2)}) async-start(), calls=%async_computation.1 | async-start | bytes 327680 | tf_op jit(solution)/shard_map/reduce_scatter | solution.py:200
  8.0 7.5 %collective-permute-start.1 = (s32[18,256]{1,0:T(8,128)S(1)}, s32[18,256]{1,0:T(8,128)S(1)}, u32[]{:S(2)}, u32[]{:S(2)}) collective-permute-start(s32[18,256]{1,0:T(8,128)S(1)} %pad_add_fusion), channel_id=1, source_target_pairs={{1,0},{2,1},{3,2},{4,3},{5,4},{6,5},{7,6},{9,8},{10,9},{11,10},{12... | collective-permute-start | bytes 55304 | tf_op jit(solution)/shard_map/ppermute | solution.py:187
  9.2 7.0 %collective-permute-start = (s32[18,256]{1,0:T(8,128)S(1)}, s32[18,256]{1,0:T(8,128)S(1)}, u32[]{:S(2)}, u32[]{:S(2)}) collective-permute-start(s32[18,256]{1,0:T(8,128)S(1)} %pad_add_fusion), channel_id=1, source_target_pairs={{0,1},{1,2},{2,3},{3,4},{4,5},{5,6},{6,7},{8,9},{9,10},{10,11},{11... | collective-permute-start | bytes 55304 | tf_op jit(solution)/shard_map/ppermute | solution.py:186
  17.7 1.6 %copy-start = (bf16[16,32,2048]{2,1,0:T(8,128)(2,1)S(1)}, bf16[16,32,2048]{2,1,0:T(8,128)(2,1)}, u32[]{:S(2)}) copy-start(bf16[16,32,2048]{2,1,0:T(8,128)(2,1)} %res_ref.1) | copy-start | bytes 6291460
  19.3 52.6 %copy-start.2 = (f32[256]{0:T(256)S(1)}, f32[256]{0:T(256)}, u32[]{:S(2)}) copy-start(f32[256]{0:T(256)} %param.15) | copy-start | bytes 3076
  19.3 52.6 %copy-start.3 = (f32[256]{0:T(256)S(1)}, f32[256]{0:T(256)}, u32[]{:S(2)}) copy-start(f32[256]{0:T(256)} %param.16) | copy-start | bytes 3076
  53.1 6.8 %collective-permute-start.2 = (f32[16896]{0:T(1024)S(1)}, f32[16896]{0:T(1024)S(1)}, u32[]{:S(2)}, u32[]{:S(2)}) collective-permute-start(f32[16896]{0:T(1024)S(1)} %pad_maximum_fusion), channel_id=1, source_target_pairs={{0,1},{1,2},{2,3},{3,4},{4,5},{5,6},{6,7},{8,9},{9,10},{10,11},{11... | collective-permute-start | bytes 202760 | tf_op jit(solution)/shard_map/ppermute | solution.py:194
  58.0 7.4 %collective-permute-start.3 = (f32[16896]{0:T(1024)S(1)}, f32[16896]{0:T(1024)S(1)}, u32[]{:S(2)}, u32[]{:S(2)}) collective-permute-start(f32[16896]{0:T(1024)S(1)} %pad_maximum_fusion.1), channel_id=1, source_target_pairs={{1,0},{2,1},{3,2},{4,3},{5,4},{6,5},{7,6},{9,8},{10,9},{11,10},{12... | collective-permute-start | bytes 202760 | tf_op jit(solution)/shard_map/ppermute | solution.py:195
  65.5 0.7 copy-start.1
Sparse Core Ops, SparseCore 0:
  66.3 21.6 reduce-scatter.1

commit v2 on v1

--- a/solution.py
+++ b/solution.py
@@ -10,9 +10,13 @@
 PAD = 8
 
 
-def local_kernel(
-    stars_ref, psf_ref, res_ref, flags_ref, grid_ref, part_ref,
+def kernel(
+    stars_ref, psf_ref, res_ref, info_ref, flux_ref, depth_ref,
+    share_ref, flux_grad_ref, depth_grad_ref,
     flat, windows, table, wide, gathered, dense, summed, split,
+    comb, part, near_stars, got_info, got_main, got_edge, got_part, got_edge_part,
+    info_send, info_recv, main_send, main_recv, edge_send, edge_recv,
+    part_send, part_recv, edge_part_send, edge_part_recv, local_sem,
 ):
     times, rows, columns = res_ref.shape
     width = psf_ref.shape[0]
@@ -21,6 +25,75 @@
     halves = rows // 16
     star_count = stars_ref.shape[1]
     tall = rows + 2 * margin
+    group_count, _, share = comb.shape
+    me = lax.axis_index("tm")
+    place_sky = lax.axis_index("sky")
+    sky_size = lax.axis_size("sky")
+    has = (place_sky > 0, place_sky < sky_size - 1)
+    beside = (place_sky - 1, place_sky + 1)
+
+    def to(tm, sky):
+        return dict(device_id={"tm": tm, "sky": sky}, device_id_type=pl.DeviceIdType.MESH)
+
+    def other(d):
+        return lax.rem(me + d, group_count)
+
+    barrier = pltpu.get_barrier_semaphore()
+    for d in range(1, group_count):
+        pl.semaphore_signal(barrier, inc=1, **to(other(d), place_sky))
+    for side in range(2):
+
+        @pl.when(has[side])
+        def _(side=side):
+            for d in range(group_count):
+                pl.semaphore_signal(barrier, inc=1, **to(other(d), beside[side]))
+
+    peers = group_count - 1
+    for side in range(2):
+        peers = peers + jnp.where(has[side], group_count, 0)
+    pl.semaphore_wait(barrier, peers)
+
+    def info_copy(side):
+        return pltpu.make_async_remote_copy(
+            src_ref=info_ref, dst_ref=got_info.at[1 - side],
+            send_sem=info_send.at[side], recv_sem=info_recv.at[1 - side],
+            **to(me, beside[side]),
+        )
+
+    def main_copy(d):
+        return pltpu.make_async_remote_copy(
+            src_ref=comb.at[other(d), pl.ds(PAD, rows)], dst_ref=got_main.at[d - 1],
+            send_sem=main_send.at[d - 1], recv_sem=main_recv.at[d - 1],
+            **to(other(d), place_sky),
+        )
+
+    def edge_copy(side, d):
+        return pltpu.make_async_remote_copy(
+            src_ref=comb.at[other(d), pl.ds((0, PAD + rows)[side], PAD)],
+            dst_ref=got_edge.at[1 - side, d],
+            send_sem=edge_send.at[side, d], recv_sem=edge_recv.at[1 - side, d],
+            **to(other(d), beside[side]),
+        )
+
+    def part_copy(d):
+        return pltpu.make_async_remote_copy(
+            src_ref=part.at[0], dst_ref=got_part.at[d - 1],
+            send_sem=part_send.at[d - 1], recv_sem=part_recv.at[d - 1],
+            **to(other(d), place_sky),
+        )
+
+    def edge_part_copy(side, d):
+        return pltpu.make_async_remote_copy(
+            src_ref=part.at[1 + side], dst_ref=got_edge_part.at[1 - side, d],
+            send_sem=edge_part_send.at[side, d], recv_sem=edge_part_recv.at[1 - side, d],
+            **to(other(d), beside[side]),
+        )
+
+    for side in range(2):
+
+        @pl.when(has[side])
+        def _(side=side):
+            info_copy(side).start()
 
     span = 144
     gap = lax.broadcasted_iota(jnp.int32, (span, LANES), 0) - lax.broadcasted_iota(
@@ -48,10 +121,10 @@
             total = total + res_ref[t, :, at].astype(jnp.float32)
         summed[:, pl.ds(pl.multiple_of((b + 1) * LANES, LANES), LANES)] = total
 
-    grid_ref[...] = jnp.zeros_like(grid_ref)
-    group = 4
-
-    @pl.loop(0, blocks // group)
+    group = share // LANES
+    comb[...] = jnp.zeros_like(comb)
+
+    @pl.loop(0, group_count)
     def _(g):
         for i in range(group):
             start = pl.multiple_of((g * group + i) * LANES, LANES)
@@ -66,11 +139,19 @@
                 split[...], wide[:, pl.ds(a * LANES, LANES)], preferred_element_type=jnp.float32
             )
             for i in range(group):
-                start = pl.multiple_of((g * group + i) * LANES, LANES)
                 term = product[2 * i * rows : (2 * i + 1) * rows] + product[
                     (2 * i + 1) * rows : (2 * i + 2) * rows
                 ]
-                grid_ref[pl.ds(PAD + margin - a, rows), pl.ds(start, LANES)] += term
+                comb[g, pl.ds(PAD + margin - a, rows), pl.ds(i * LANES, LANES)] += term
+
+    for d in range(1, group_count):
+        main_copy(d).start()
+    for side in range(2):
+
+        @pl.when(has[side])
+        def _(side=side):
+            for d in range(group_count):
+                edge_copy(side, d).start()
 
     flat[:, pl.ds(0, LANES)] = jnp.zeros((256, LANES), jnp.float32)
     flat[:, pl.ds(LANES + columns, LANES)] = jnp.zeros((256, LANES), jnp.float32)
@@ -103,17 +184,17 @@
             windows[blocks + b, rows_at] = far.astype(jnp.bfloat16).reshape(16, 16, LANES)
 
     lane = lax.broadcasted_iota(jnp.int32, (16, LANES), 1)
-    lowest = lax.axis_index("sky") * rows
-    for which, (first_tap, taps) in enumerate(((0, width), (width - margin, margin), (0, margin))):
-        base = first_tap
+    lowest = place_sky * rows
+    part[...] = jnp.zeros_like(part)
+
+    def stars_part(which, first_tap, taps, star_row, star_col, flags):
         last = tall - taps
 
         def chunk(g, c, slot, acc):
             for s in range(16):
                 star = g * LANES + c * 16 + s
-                row = stars_ref[2 * which, star] - lowest + base
-                row = jnp.clip(row, 0, last)
-                column = stars_ref[2 * which + 1, star]
+                row = jnp.clip(star_row(star) - lowest + first_tap, 0, last)
+                column = star_col(star)
                 block = column // LANES + blocks * ((column // 64) % 2)
                 found = windows[block, pl.ds(row, taps)]
                 for a in range(taps):
@@ -126,7 +207,7 @@
             for s in range(16):
                 star = g * LANES + c * 16 + s
                 place = c * 16 + s
-                offset = stars_ref[2 * which + 1, star] % 64
+                offset = star_col(star) % 64
                 moved = pltpu.roll(
                     dense[slot, pl.ds(16 * s, 16), :], (place - offset + LANES) % LANES, 1
                 )
@@ -141,28 +222,109 @@
 
             acc = lax.fori_loop(0, LANES // 32, pair, jnp.zeros((16, LANES), jnp.float32))
             at = pl.ds(g * LANES, LANES)
-            part_ref[pl.ds(2 * which, 1), at] = jnp.sum(acc, axis=0, keepdims=True)
-            part_ref[pl.ds(2 * which + 1, 1), at] = jnp.sum(
-                acc * flags_ref[which, :, at], axis=0, keepdims=True
-            )
-
-
-def local_parts(stars, spread, residual, flags):
+            part[which, pl.ds(0, 1), at] = jnp.sum(acc, axis=0, keepdims=True)
+            part[which, pl.ds(1, 1), at] = jnp.sum(
+                acc * flags(at).astype(jnp.float32), axis=0, keepdims=True
+            )
+
+    stars_part(
+        0, 0, width,
+        lambda n: stars_ref[0, n], lambda n: stars_ref[1, n],
+        lambda at: info_ref[pl.ds(8, times), at],
+    )
+    for d in range(1, group_count):
+        part_copy(d).start()
+    for side in range(2):
+
+        @pl.when(has[side])
+        def _(side=side):
+            info_copy(1 - side).wait_recv()
+            fetch = pltpu.make_async_copy(
+                got_info.at[side, pl.ds(0, 8)], near_stars.at[side], local_sem
+            )
+            fetch.start()
+            fetch.wait()
+            stars_part(
+                1 + side, (width - margin, 0)[side], margin,
+                lambda n: near_stars[side, 0, n], lambda n: near_stars[side, 1, n],
+                lambda at: got_info[side, pl.ds(8, times), at],
+            )
+            for d in range(group_count):
+                edge_part_copy(side, d).start()
+
+    for d in range(1, group_count):
+        main_copy(d).wait_recv()
+    total = comb[me, pl.ds(PAD, rows)]
+    for d in range(1, group_count):
+        total = total + got_main[d - 1]
+    share_ref[...] = total
+    for side in range(2):
+
+        @pl.when(has[side])
+        def _(side=side):
+            for d in range(group_count):
+                edge_copy(1 - side, d).wait_recv()
+            edge = got_edge[side, 0]
+            for d in range(1, group_count):
+                edge = edge + got_edge[side, d]
+            share_ref[pl.ds((0, rows - PAD)[side], PAD), :] += edge
+
+    for d in range(1, group_count):
+        part_copy(d).wait_recv()
+    sums = part[0]
+    for d in range(1, group_count):
+        sums = sums + got_part[d - 1]
+    flux_grad_ref[...] = sums[0:1]
+    depth_grad_ref[...] = sums[1:2]
+    for side in range(2):
+
+        @pl.when(has[side])
+        def _(side=side):
+            for d in range(group_count):
+                edge_part_copy(1 - side, d).wait_recv()
+            edge = got_edge_part[side, 0]
+            for d in range(1, group_count):
+                edge = edge + got_edge_part[side, d]
+            flux_grad_ref[...] += edge[0:1]
+            depth_grad_ref[...] += edge[1:2]
+
+    flux_grad_ref[...] = flux_grad_ref[...] - depth_ref[...] * depth_grad_ref[...]
+    depth_grad_ref[...] = -flux_ref[...] * depth_grad_ref[...]
+    for d in range(1, group_count):
+        main_copy(d).wait_send()
+        part_copy(d).wait_send()
+    for side in range(2):
+
+        @pl.when(has[side])
+        def _(side=side):
+            info_copy(side).wait_send()
+            for d in range(group_count):
+                edge_copy(side, d).wait_send()
+                edge_part_copy(side, d).wait_send()
+
+
+def per_device(residual, point_spread, star_row, star_col, star_flux, transit_depth, transit_flag):
     times, rows, columns = residual.shape
-    width = spread.shape[0]
+    width = point_spread.shape[0]
     margin = (width - 1) // 2
     blocks = columns // LANES
-    count = stars.shape[1]
+    count = star_row.shape[0]
+    groups = lax.axis_size("tm")
+    share = columns // groups
+    stars = jnp.stack([star_row, star_col])
+    info = jnp.concatenate([stars, jnp.zeros((6, count), jnp.int32), transit_flag], axis=0)
     vmem = pl.BlockSpec(memory_space=pltpu.VMEM)
     smem = pl.BlockSpec(memory_space=pltpu.SMEM)
-    return pl.pallas_call(
-        local_kernel,
+    dma = pltpu.SemaphoreType.DMA
+    grid_share, flux_grad, depth_grad = pl.pallas_call(
+        kernel,
         out_shape=(
-            jax.ShapeDtypeStruct((rows + 2 * PAD, columns), jnp.float32),
-            jax.ShapeDtypeStruct((8, count), jnp.float32),
+            jax.ShapeDtypeStruct((rows, share), jnp.float32),
+            jax.ShapeDtypeStruct((1, count), jnp.float32),
+            jax.ShapeDtypeStruct((1, count), jnp.float32),
         ),
-        in_specs=[smem, smem, vmem, vmem],
-        out_specs=(vmem, vmem),
+        in_specs=[smem, smem, vmem, vmem, vmem, vmem],
+        out_specs=(vmem, vmem, vmem),
         scratch_shapes=[
             pltpu.VMEM((256, columns + 2 * LANES), jnp.float32),
             pltpu.VMEM((2 * blocks, rows + 2 * margin, 16, LANES), jnp.bfloat16),
@@ -171,35 +333,24 @@
             pltpu.VMEM((2, 256, width * LANES), jnp.bfloat16),
             pltpu.VMEM((2, 256, LANES), jnp.float32),
             pltpu.VMEM((rows, columns + 3 * LANES), jnp.float32),
-            pltpu.VMEM((8 * rows, 256), jnp.bfloat16),
+            pltpu.VMEM((2 * rows * (share // LANES), 256), jnp.bfloat16),
+            pltpu.VMEM((groups, rows + 2 * PAD, share), jnp.float32),
+            pltpu.VMEM((3, 8, count), jnp.float32),
+            pltpu.SMEM((2, 8, count), jnp.int32),
+            pltpu.VMEM((2, 8 + times, count), jnp.int32),
+            pltpu.VMEM((groups - 1, rows, share), jnp.float32),
+            pltpu.VMEM((2, groups, PAD, share), jnp.float32),
+            pltpu.VMEM((groups - 1, 8, count), jnp.float32),
+            pltpu.VMEM((2, groups, 8, count), jnp.float32),
+            dma((2,)), dma((2,)), dma((groups - 1,)), dma((groups - 1,)),
+            dma((2, groups)), dma((2, groups)), dma((groups - 1,)), dma((groups - 1,)),
+            dma((2, groups)), dma((2, groups)), dma,
         ],
-        compiler_params=pltpu.CompilerParams(vmem_limit_bytes=40 << 20),
-    )(stars, spread, residual, flags)
-
-
-def per_device(residual, point_spread, star_row, star_col, star_flux, transit_depth, transit_flag):
-    times, rows, columns = residual.shape
-    size = lax.axis_size("sky")
-    up = [(i, i + 1) for i in range(size - 1)]
-    down = [(i + 1, i) for i in range(size - 1)]
-    info = jnp.concatenate([star_row[None], star_col[None], transit_flag], axis=0)
-    before = lax.ppermute(info, "sky", up)
-    after = lax.ppermute(info, "sky", down)
-    stars = jnp.concatenate([info[:2], before[:2], after[:2]], axis=0)
-    flags = jnp.stack([info[2:], before[2:], after[2:]]).astype(jnp.float32)
-    grid, part = local_parts(stars, point_spread.astype(jnp.float32), residual, flags)
-    edge_count = PAD * columns
-    to_before = jnp.concatenate([grid[:PAD].reshape(-1), part[2:4].reshape(-1)])
-    to_after = jnp.concatenate([grid[PAD + rows :].reshape(-1), part[4:6].reshape(-1)])
-    from_before = lax.ppermute(to_after, "sky", up)
-    from_after = lax.ppermute(to_before, "sky", down)
-    own = grid[PAD : PAD + rows]
-    own = own.at[:PAD].add(from_before[:edge_count].reshape(PAD, columns))
-    own = own.at[rows - PAD :].add(from_after[:edge_count].reshape(PAD, columns))
-    sums = part[:2] + (from_before[edge_count:] + from_after[edge_count:]).reshape(2, -1)
-    grid_share = lax.psum_scatter(own, "tm", scatter_dimension=1, tiled=True)
-    sums = lax.psum(sums, "tm")
-    return (grid_share, sums[0] - transit_depth * sums[1], -star_flux * sums[1])
+        compiler_params=pltpu.CompilerParams(
+            collective_id=0, has_side_effects=True, vmem_limit_bytes=48 << 20
+        ),
+    )(stars, point_spread.astype(jnp.float32), residual, info, star_flux[None], transit_depth[None])
+    return grid_share, flux_grad[0], depth_grad[0]
 
 
 def solution(mesh):

time: 95.3 us -> 49.4 us (0.52)
  the two profiles are of different devices: /device:TPU:0 before, /device:TPU:9 now
where the time goes in v2:
time: 49.4 us; the launch traced here: 49.2 us
  Pallas kernels  41.5 us (84%)
  local copies, waits for them, and re-layouts  4.78 us (10%)
  other arithmetic  2.2 us (4%)
  between operations  0.65 us (1%)
    pallas_call x1, Pallas kernels, per_device(): pl.pallas_call(kernel, out_shape=(jax.ShapeDtypeStruct((rows, share), jnp...  41.5 us
    unnamed x9, local copies, waits for them, and re-layouts  4.71 us

profile of v2, /device:TPU:9, one launch (start us, length us, event | category | flops | bytes accessed | tf_op | source)
XLA Modules:
  0.0 49.2 jit_solution(4867494561501283065)
XLA Ops:
  0.6 0.1 pad.2.clone
  0.7 0.7 %pad_add_fusion.1.stars_ref = s32[2,256]{1,0:T(2,128)S(1)} fusion(s32[1,256]{1,0:T(1,128)} %bitcast.10, s32[1,256]{1,0:T(1,128)} %bitcast.12), kind=kLoop, calls=%fused_computation.1 | loop fusion | flops 512 | bytes 4096 | tf_op jit(solution)/shard_map/stack | solution.py:314
  1.4 0.7 %convert_element_type.3.psf_ref = f32[11,11]{1,0:T(8,128)S(1)} convert(bf16[11,11]{1,0:T(8,128)(2,1)} %param.8) | non-fusion elementwise | flops 121 | bytes 726 | tf_op jit(solution)/shard_map/convert_element_type | solution.py:352
  2.1 0.8 %pad_add_fusion.info_ref = s32[24,256]{1,0:T(8,128)S(1)} fusion(s32[16,256]{1,0:T(8,128)} %param.13, s32[1,256]{1,0:T(1,128)} %bitcast.11, s32[1,256]{1,0:T(1,128)} %bitcast.13, s32[24]{0:T(128)S(1)} %pad.2.clone), kind=kLoop, calls=%fused_computation | loop fusion | flops 18432 | bytes 43104 | tf_op jit(solution)/shard_map/concatenate | solution.py:315
  2.9 0.0 copy-start
  2.9 1.6 %copy-done = bf16[16,32,2048]{2,1,0:T(8,128)(2,1)S(1)} copy-done((bf16[16,32,2048]{2,1,0:T(8,128)(2,1)S(1)}, bf16[16,32,2048]{2,1,0:T(8,128)(2,1)}, u32[]{:S(2)}) %copy-start) | copy-done | bytes 2097176
  4.5 0.0 copy-start.1
  4.5 0.7 %copy-done.1 = f32[256]{0:T(256)S(1)} copy-done((f32[256]{0:T(256)S(1)}, f32[256]{0:T(256)}, u32[]{:S(2)}) %copy-start.1) | copy-done | bytes 1048
  5.2 0.0 copy-start.2
  5.2 0.7 %copy-done.2 = f32[256]{0:T(256)S(1)} copy-done((f32[256]{0:T(256)S(1)}, f32[256]{0:T(256)}, u32[]{:S(2)}) %copy-start.2) | copy-done | bytes 1048
  5.9 41.5 %shard_map.94 = (f32[32,512]{1,0:T(8,128)S(1)}, f32[1,256]{1,0:T(1,128)S(1)}, f32[1,256]{1,0:T(1,128)S(1)}) custom-call(s32[2,256]{1,0:T(2,128)S(1)} %pad_add_fusion.1.stars_ref, f32[11,11]{1,0:T(8,128)S(1)} %convert_element_type.3.psf_ref, bf16[16,32,2048]{2,1,0:T(8,128)(2,1)S(1)} %copy-done, s32[24,256]{1,0:T(8,128)S(1)} %pad_add_fusion.info_ref, ...), custom_call_target="tpu_custom_call" | custom-call | tf_op jit(solution)/shard_map/pallas_call | solution.py:319
  47.4 0.6 %copy.13 = f32[32,512]{1,0:T(8,128)} copy(f32[32,512]{1,0:T(8,128)S(1)} %get-tuple-element.12) | data formatting | bytes 131072
  48.0 0.6 %copy.14 = f32[256]{0:T(256)} copy(f32[256]{0:T(256)S(1)} %bitcast.9) | data formatting | bytes 2048
  48.6 0.6 %copy.15 = f32[256]{0:T(256)} copy(f32[256]{0:T(256)S(1)} %bitcast.8) | data formatting | bytes 2048
  (1 shorter events, 0.0 us)
Async XLA Ops:
  2.9 1.6 %copy-start = (bf16[16,32,2048]{2,1,0:T(8,128)(2,1)S(1)}, bf16[16,32,2048]{2,1,0:T(8,128)(2,1)}, u32[]{:S(2)}) copy-start(bf16[16,32,2048]{2,1,0:T(8,128)(2,1)} %res_ref.1) | copy-start | bytes 6291460
  4.5 0.7 %copy-start.1 = (f32[256]{0:T(256)S(1)}, f32[256]{0:T(256)}, u32[]{:S(2)}) copy-start(f32[256]{0:T(256)} %param.11) | copy-start | bytes 3076
  5.2 0.7 %copy-start.2 = (f32[256]{0:T(256)S(1)}, f32[256]{0:T(256)}, u32[]{:S(2)}) copy-start(f32[256]{0:T(256)} %param.12) | copy-start | bytes 3076

commit v3 on v2

v3 whole, which is shorter than its diff:
```python
import functools
import jax
import jax.numpy as jnp
from jax import lax
from jax.experimental import pallas as pl
from jax.experimental.pallas import tpu as pltpu
from jax.sharding import PartitionSpec as P

LANES = 128
PAD = 8


def kernel(
    psf_hbm, res_hbm, row_hbm, col_hbm, flag_hbm,
    share_ref, plain_ref, flagged_ref,
    psf_ref, res_ref, stars, flags, codes, lookup,
    flat, windows, table, wide, gathered, dense, summed, split,
    comb, part, got_main, got_edge, got_part, got_edge_part,
    info_send, info_recv, main_send, main_recv, edge_send, edge_recv,
    part_send, part_recv, edge_part_send, edge_part_recv, local_sem, lookup_sem,
):
    times, rows, columns = res_ref.shape
    width = psf_ref.shape[0]
    margin = (width - 1) // 2
    blocks = columns // LANES
    halves = rows // 16
    star_count = row_hbm.shape[1]
    tall = rows + 2 * margin
    group_count, _, share = comb.shape
    me = lax.axis_index("tm")
    place_sky = lax.axis_index("sky")
    sky_size = lax.axis_size("sky")
    has = (place_sky > 0, place_sky < sky_size - 1)
    beside = (place_sky - 1, place_sky + 1)

    def to(tm, sky):
        return dict(device_id={"tm": tm, "sky": sky}, device_id_type=pl.DeviceIdType.MESH)

    def other(d):
        return lax.rem(me + d, group_count)

    barrier = pltpu.get_barrier_semaphore()
    for d in range(1, group_count):
        pl.semaphore_signal(barrier, inc=1, **to(other(d), place_sky))
    for side in range(2):

        @pl.when(has[side])
        def _(side=side):
            for d in range(group_count):
                pl.semaphore_signal(barrier, inc=1, **to(other(d), beside[side]))

    loads = [
        pltpu.make_async_copy(source, target, local_sem.at[n])
        for n, (source, target) in enumerate(
            (
                (psf_hbm, psf_ref),
                (row_hbm, stars.at[0, 0]),
                (col_hbm, stars.at[0, 1]),
                (flag_hbm, flags.at[0]),
                (res_hbm, res_ref),
            )
        )
    ]
    for load in loads:
        load.start()

    peers = group_count - 1
    for side in range(2):
        peers = peers + jnp.where(has[side], group_count, 0)
    pl.semaphore_wait(barrier, peers)

    def info_copies(side):
        other_side = 1 - side
        return [
            pltpu.make_async_remote_copy(
                src_ref=source, dst_ref=target,
                send_sem=info_send.at[side, n], recv_sem=info_recv.at[other_side, n],
                **to(me, beside[side]),
            )
            for n, (source, target) in enumerate(
                (
                    (row_hbm, stars.at[1 + other_side, 0]),
                    (col_hbm, stars.at[1 + other_side, 1]),
                    (flag_hbm, flags.at[1 + other_side]),
                )
            )
        ]

    def main_copy(d):
        return pltpu.make_async_remote_copy(
            src_ref=comb.at[other(d), pl.ds(PAD, rows)], dst_ref=got_main.at[d - 1],
            send_sem=main_send.at[d - 1], recv_sem=main_recv.at[d - 1],
            **to(other(d), place_sky),
        )

    def edge_copy(side, d):
        return pltpu.make_async_remote_copy(
            src_ref=comb.at[other(d), pl.ds((0, PAD + rows)[side], PAD)],
            dst_ref=got_edge.at[1 - side, d],
            send_sem=edge_send.at[side, d], recv_sem=edge_recv.at[1 - side, d],
            **to(other(d), beside[side]),
        )

    def part_copy(d):
        return pltpu.make_async_remote_copy(
            src_ref=part.at[0], dst_ref=got_part.at[d - 1],
            send_sem=part_send.at[d - 1], recv_sem=part_recv.at[d - 1],
            **to(other(d), place_sky),
        )

    def edge_part_copy(side, d):
        return pltpu.make_async_remote_copy(
            src_ref=part.at[1 + side], dst_ref=got_edge_part.at[1 - side, d],
            send_sem=edge_part_send.at[side, d], recv_sem=edge_part_recv.at[1 - side, d],
            **to(other(d), beside[side]),
        )

    for side in range(2):

        @pl.when(has[side])
        def _(side=side):
            for copy in info_copies(side):
                copy.start()

    lowest = place_sky * rows

    def taps_of(which):
        return ((0, width), (width - margin, margin), (0, margin))[which]

    def look_up(which):
        first_tap, taps = taps_of(which)
        row = jnp.clip(stars[which, 0] - lowest + first_tap, 0, tall - taps)
        column = stars[which, 1]
        block = lax.shift_right_logical(column, 7) + blocks * (
            lax.shift_right_logical(column, 6) & 1
        )
        codes[which, 0] = block * tall + row
        position = lax.broadcasted_iota(jnp.int32, (1, star_count), 1)
        codes[which, 1] = (position - (column & 63)) & (LANES - 1)
        return pltpu.make_async_copy(codes.at[which], lookup.at[which], lookup_sem.at[which])

    loads[1].wait()
    loads[2].wait()
    own_lookup = look_up(0)
    own_lookup.start()
    loads[0].wait()
    spread = psf_ref[...].astype(jnp.float32)

    span = 144
    gap = lax.broadcasted_iota(jnp.int32, (span, LANES), 0) - lax.broadcasted_iota(
        jnp.int32, (span, LANES), 1
    )
    for a in range(width):
        entry = jnp.zeros((span, LANES), jnp.float32)
        for b in range(width):
            entry = jnp.where(gap == b, spread[a : a + 1, b : b + 1], entry)
        entry = entry.astype(jnp.bfloat16)
        table[pl.ds(a * LANES, LANES), :] = entry[:LANES]
        wide[pl.ds(0, span), pl.ds(a * LANES, LANES)] = entry
    wide[pl.ds(span, 256 - span), :] = jnp.zeros((256 - span, width * LANES), jnp.bfloat16)

    loads[4].wait()
    zero_side = jnp.zeros((rows, LANES), jnp.float32)
    summed[:, pl.ds(0, LANES)] = zero_side
    summed[:, pl.ds(LANES + columns, LANES)] = zero_side
    summed[:, pl.ds(2 * LANES + columns, LANES)] = zero_side

    @pl.loop(0, blocks)
    def _(b):
        at = pl.ds(pl.multiple_of(b * LANES, LANES), LANES)
        total = res_ref[0, :, at].astype(jnp.float32)
        for t in range(1, times):
            total = total + res_ref[t, :, at].astype(jnp.float32)
        summed[:, pl.ds(pl.multiple_of((b + 1) * LANES, LANES), LANES)] = total

    group = share // LANES
    comb[...] = jnp.zeros_like(comb)

    @pl.loop(0, group_count)
    def _(g):
        for i in range(group):
            start = pl.multiple_of((g * group + i) * LANES, LANES)
            window = summed[:, pl.ds(start, 3 * LANES)]
            moved = pltpu.roll(window, margin, 1)[:, LANES:]
            high = moved.astype(jnp.bfloat16)
            low = (moved - high.astype(jnp.float32)).astype(jnp.bfloat16)
            split[pl.ds(2 * i * rows, rows), :] = high
            split[pl.ds((2 * i + 1) * rows, rows), :] = low
        for a in range(width):
            product = jnp.dot(
                split[...], wide[:, pl.ds(a * LANES, LANES)], preferred_element_type=jnp.float32
            )
            for i in range(group):
                term = product[2 * i * rows : (2 * i + 1) * rows] + product[
                    (2 * i + 1) * rows : (2 * i + 2) * rows
                ]
                comb[g, pl.ds(PAD + margin - a, rows), pl.ds(i * LANES, LANES)] += term

    for d in range(1, group_count):
        main_copy(d).start()
    for side in range(2):

        @pl.when(has[side])
        def _(side=side):
            for d in range(group_count):
                edge_copy(side, d).start()

    flat[:, pl.ds(0, LANES)] = jnp.zeros((256, LANES), jnp.float32)
    flat[:, pl.ds(LANES + columns, LANES)] = jnp.zeros((256, LANES), jnp.float32)
    first = lax.broadcasted_iota(jnp.int32, (256, 256), 0)
    second = lax.broadcasted_iota(jnp.int32, (256, 256), 1)
    swap = (first == (second % 16) * 16 + second // 16).astype(jnp.bfloat16)
    for b in range(2 * blocks):
        for r in (b * tall, b * tall + margin + rows):
            windows[pl.ds(r, margin)] = jnp.zeros((margin, 16, LANES), jnp.bfloat16)
    for h in range(halves):

        @pl.loop(0, columns // 256)
        def _(c):
            at = pl.ds(pl.multiple_of(c * 256, 256), 256)
            piece = res_ref[:, pl.ds(16 * h, 16), at].reshape(256, 256)
            flat[:, pl.ds(pl.multiple_of(c * 256 + LANES, LANES), 256)] = jnp.dot(
                swap, piece, preferred_element_type=jnp.float32
            )

        @pl.loop(0, blocks // 4)
        def _(c):
            start = pl.multiple_of(c * 4 * LANES, LANES)
            left = flat[:, pl.ds(start, 5 * LANES)]
            right = flat[:, pl.ds(pl.multiple_of(start + LANES, LANES), 5 * LANES)]
            near = pltpu.roll(left, margin, 1).astype(jnp.bfloat16)
            far = pltpu.roll(right, 5 * LANES - (64 - margin), 1).astype(jnp.bfloat16)
            for i in range(4):
                b = c * 4 + i
                windows[pl.ds(b * tall + margin + 16 * h, 16)] = near[
                    :, (i + 1) * LANES : (i + 2) * LANES
                ].reshape(16, 16, LANES)
                windows[pl.ds((blocks + b) * tall + margin + 16 * h, 16)] = far[
                    :, i * LANES : (i + 1) * LANES
                ].reshape(16, 16, LANES)

    lane = lax.broadcasted_iota(jnp.int32, (16, LANES), 1)
    part[...] = jnp.zeros_like(part)
    slots = gathered.shape[0]

    def stars_part(which):
        first_tap, taps = taps_of(which)
        for g in range(star_count // LANES):

            def gather(c, slot, g=g):
                for s in range(16):
                    found = windows[pl.ds(lookup[which, 0, 0, g * LANES + c * 16 + s], taps)]
                    for a in range(taps):
                        gathered[slot, pl.ds(16 * s, 16), pl.ds(a * LANES, LANES)] = found[a]

            def multiply(slot):
                dense[slot] = jnp.dot(
                    gathered[slot, :, pl.ds(0, taps * LANES)],
                    table[pl.ds(first_tap * LANES, taps * LANES), :],
                    preferred_element_type=jnp.float32,
                )

            def select(c, slot, acc, g=g):
                for s in range(16):
                    moved = pltpu.roll(
                        dense[slot, pl.ds(16 * s, 16), :],
                        lookup[which, 1, 0, g * LANES + c * 16 + s],
                        1,
                    )
                    acc = jnp.where(lane == c * 16 + s, moved, acc)
                return acc

            def some(c, acc):
                for n in range(slots + 2):
                    if n < slots:
                        gather(slots * c + n, n)
                        multiply(n)
                    if n >= 2:
                        acc = select(slots * c + n - 2, n - 2, acc)
                return acc

            acc = lax.fori_loop(
                0, LANES // (16 * slots), some, jnp.zeros((16, LANES), jnp.float32)
            )
            at = pl.ds(g * LANES, LANES)
            part[which, pl.ds(0, 1), at] = jnp.sum(acc, axis=0, keepdims=True)
            part[which, pl.ds(1, 1), at] = jnp.sum(
                acc * flags[which, :, at].astype(jnp.float32), axis=0, keepdims=True
            )

    own_lookup.wait()
    loads[3].wait()
    stars_part(0)
    for d in range(1, group_count):
        part_copy(d).start()
    for side in range(2):

        @pl.when(has[side])
        def _(side=side):
            for copy in info_copies(1 - side):
                copy.wait_recv()
            near_lookup = look_up(1 + side)
            near_lookup.start()
            near_lookup.wait()
            stars_part(1 + side)
            for d in range(group_count):
                edge_part_copy(side, d).start()

    for d in range(1, group_count):
        main_copy(d).wait_recv()
    total = comb[me, pl.ds(PAD, rows)]
    for d in range(1, group_count):
        total = total + got_main[d - 1]
    share_ref[...] = total
    for side in range(2):

        @pl.when(has[side])
        def _(side=side):
            for d in range(group_count):
                edge_copy(1 - side, d).wait_recv()
            edge = got_edge[side, 0]
            for d in range(1, group_count):
                edge = edge + got_edge[side, d]
            share_ref[pl.ds((0, rows - PAD)[side], PAD), :] += edge

    for d in range(1, group_count):
        part_copy(d).wait_recv()
    sums = part[0]
    for d in range(1, group_count):
        sums = sums + got_part[d - 1]
    plain_ref[...] = sums[0:1]
    flagged_ref[...] = sums[1:2]
    for side in range(2):

        @pl.when(has[side])
        def _(side=side):
            for d in range(group_count):
                edge_part_copy(1 - side, d).wait_recv()
            edge = got_edge_part[side, 0]
            for d in range(1, group_count):
                edge = edge + got_edge_part[side, d]
            plain_ref[...] += edge[0:1]
            flagged_ref[...] += edge[1:2]

    for d in range(1, group_count):
        main_copy(d).wait_send()
        part_copy(d).wait_send()
    for side in range(2):

        @pl.when(has[side])
        def _(side=side):
            for copy in info_copies(side):
                copy.wait_send()
            for d in range(group_count):
                edge_copy(side, d).wait_send()
                edge_part_copy(side, d).wait_send()


def per_device(residual, point_spread, star_row, star_col, star_flux, transit_depth, transit_flag):
    times, rows, columns = residual.shape
    width = point_spread.shape[0]
    margin = (width - 1) // 2
    blocks = columns // LANES
    count = star_row.shape[0]
    groups = lax.axis_size("tm")
    share = columns // groups
    vmem = pl.BlockSpec(memory_space=pltpu.VMEM)
    anywhere = pl.BlockSpec(memory_space=pltpu.HBM)
    dma = pltpu.SemaphoreType.DMA
    grid_share, plain, flagged = pl.pallas_call(
        kernel,
        out_shape=(
            jax.ShapeDtypeStruct((rows, share), jnp.float32),
            jax.ShapeDtypeStruct((1, count), jnp.float32),
            jax.ShapeDtypeStruct((1, count), jnp.float32),
        ),
        in_specs=[anywhere] * 5,
        out_specs=(vmem, vmem, vmem),
        scratch_shapes=[
            pltpu.VMEM(point_spread.shape, point_spread.dtype),
            pltpu.VMEM(residual.shape, residual.dtype),
            pltpu.VMEM((3, 2, 1, count), jnp.int32),
            pltpu.VMEM((3, times, count), jnp.int32),
            pltpu.VMEM((3, 2, 1, count), jnp.int32),
            pltpu.SMEM((3, 2, 1, count), jnp.int32),
            pltpu.VMEM((256, columns + 2 * LANES), jnp.float32),
            pltpu.VMEM((2 * blocks * (rows + 2 * margin), 16, LANES), jnp.bfloat16),
            pltpu.VMEM((width * LANES, LANES), jnp.bfloat16),
            pltpu.VMEM((256, width * LANES), jnp.bfloat16),
            pltpu.VMEM((4, 256, width * LANES), jnp.bfloat16),
            pltpu.VMEM((4, 256, LANES), jnp.float32),
            pltpu.VMEM((rows, columns + 3 * LANES), jnp.float32),
            pltpu.VMEM((2 * rows * (share // LANES), 256), jnp.bfloat16),
            pltpu.VMEM((groups, rows + 2 * PAD, share), jnp.float32),
            pltpu.VMEM((3, 8, count), jnp.float32),
            pltpu.VMEM((groups - 1, rows, share), jnp.float32),
            pltpu.VMEM((2, groups, PAD, share), jnp.float32),
            pltpu.VMEM((groups - 1, 8, count), jnp.float32),
            pltpu.VMEM((2, groups, 8, count), jnp.float32),
            dma((2, 3)), dma((2, 3)), dma((groups - 1,)), dma((groups - 1,)),
            dma((2, groups)), dma((2, groups)), dma((groups - 1,)), dma((groups - 1,)),
            dma((2, groups)), dma((2, groups)), dma((5,)), dma((3,)),
        ],
        compiler_params=pltpu.CompilerParams(
            collective_id=0, has_side_effects=True, vmem_limit_bytes=62 << 20
        ),
    )(point_spread, residual, star_row[None], star_col[None], transit_flag)
    return grid_share, plain[0] - transit_depth * flagged[0], -star_flux * flagged[0]


def solution(mesh):
    in_specs = (P("tm", "sky", None), P(), P("sky"), P("sky"), P("sky"), P("sky"), P("tm", "sky"))
    out_specs = (P("sky", "tm"), P("sky"), P("sky"))
    return jax.shard_map(
        per_device, mesh=mesh, in_specs=in_specs, out_specs=out_specs, check_vma=False
    )
```

time: 49.4 us -> 31.4 us (0.64)
  Pallas kernels: 41.5 us -> 27.8 us
  local copies, waits for them, and re-layouts: 4.78 us -> 1.48 us
  other arithmetic: 2.2 us -> 1.24 us
    pallas_call x1, Pallas kernels: 41.5 us -> 27.8 us  [per_device(): pl.pallas_call(kernel, out_shape=(jax.ShapeDtypeStruct((rows, share), jnp...]
    unnamed x9 -> x5, local copies, waits for them, and re-layouts: 4.71 us -> 1.48 us
    mul x0 -> x1, other arithmetic: none -> 1.24 us  [per_device(): -star_flux * flagged[0]]
    concatenate x1 -> x0, other arithmetic: 0.81 us -> none  [per_device(): jnp.concatenate([stars, jnp.zeros((6, count), jnp.int32), transit_flag],...]
    another operation x1 -> x0, other arithmetic: 0.7 us -> none  [per_device(): stars = jnp.stack([star_row, star_col])]
    convert_element_type x1 -> x0, other arithmetic: 0.69 us -> none  [per_device(): point_spread.astype(jnp.float32)]
where the time goes in v3:
time: 31.4 us; the launch traced here: 31.2 us
  Pallas kernels  27.8 us (89%)
  local copies, waits for them, and re-layouts  1.48 us (5%)
  other arithmetic  1.24 us (4%)
  between operations  0.67 us (2%)
    pallas_call x1, Pallas kernels, per_device(): pl.pallas_call(kernel, out_shape=(jax.ShapeDtypeStruct((rows, share), jnp...  27.8 us
    unnamed x5, local copies, waits for them, and re-layouts  1.48 us
    mul x1, other arithmetic, per_device(): -star_flux * flagged[0]  1.24 us

profile of v3, /device:TPU:9, one launch (start us, length us, event | category | flops | bytes accessed | tf_op | source)
XLA Modules:
  0.0 31.2 jit_solution(10694439638860825768)
XLA Ops:
  0.6 0.0 copy-start.1
  0.6 0.0 copy-start
  0.7 27.8 %shard_map.94 = (f32[32,512]{1,0:T(8,128)}, f32[1,256]{1,0:T(1,128)}, f32[1,256]{1,0:T(1,128)}) custom-call(bf16[11,11]{1,0:T(8,128)(2,1)} %psf_hbm.1, bf16[16,32,2048]{2,1,0:T(8,128)(2,1)} %res_hbm.1, s32[1,256]{1,0:T(1,128)} %bitcast.4, s32[1,256]{1,0:T(1,128)} %bitcast.5, s32[16,256]{1,0:T(8,128)} %flag_hbm.1), custom_call_target="tpu_custom_call" | custom-call | tf_op jit(solution)/shard_map/pallas_call | solution.py:370
  28.5 0.0 copy-done.1
  28.5 0.0 copy-done
  28.5 1.2 %negate_multiply_fusion = (f32[256]{0:T(256)}, f32[256]{0:T(256)}) fusion(f32[256]{0:T(256)} %bitcast.7, f32[256]{0:T(256)S(1)} %copy-done, f32[256]{0:T(256)} %bitcast.6, f32[256]{0:T(256)S(1)} %copy-done.1), kind=kLoop, calls=%fused_computation | loop fusion | flops 1024 | bytes 6144 | tf_op jit(solution)/shard_map/mul | solution.py:408
  29.8 1.5 %copy.11 = f32[32,512]{1,0:T(8,128)} copy(f32[32,512]{1,0:T(8,128)} %get-tuple-element.14) | data formatting | bytes 131072
Async XLA Ops:
  0.6 27.9 %copy-start.1 = (f32[256]{0:T(256)S(1)}, f32[256]{0:T(256)}, u32[]{:S(2)}) copy-start(f32[256]{0:T(256)} %param.12) | copy-start | bytes 3076
  0.6 27.9 %copy-start = (f32[256]{0:T(256)S(1)}, f32[256]{0:T(256)}, u32[]{:S(2)}) copy-start(f32[256]{0:T(256)} %param.11) | copy-start | bytes 3076
